TPU v7x, 32 devices: a whole 2x2x4 slice. The times are simulated.
32 devices in a mesh: cand: 4 (over x, core), seq: 8 (over z, y).
Axes of the slice: x: 2, y: 2, z: 4, core: 2. Of those that a mesh axis runs over, the one named last changes fastest.
Arguments:
- latent: bfloat16 [4, 384, 3072], P('cand', 'seq'), may hold values from -0.59765625 to 0.59765625
- timesteps: int32 [4], replicated, may hold values from 0 to 999
- positions: int32 [3, 384], replicated, may hold values from 0 to 63
- mod_weight: bfloat16 [3072, 9216], P('cand', 'seq'), may hold values from -0.109375 to 0.109375
- input_weight: bfloat16 [3072, 16, 384], P('cand', 'seq'), may hold values from -0.109375 to 0.109375
- output_weight: bfloat16 [16, 128, 3072], P('seq', None, 'cand'), may hold values from -0.75 to 0.75
- cotangent: bfloat16 [4, 384, 3072], P('cand', 'seq'), may hold values from -6 to 6
Outputs:
- block_out: bfloat16 [4, 384, 3072], P('cand', 'seq')
- latent_grad: float32 [4, 384, 3072], P('cand', 'seq')
All inputs are finite; a program needn't handle non-finite values.
Results may differ from a plain program's by a relative error of at most 0.033.
Values may be sent and summed in bfloat16 or wider, within the bound.
A program may use at most 128 MiB of HBM per device.

v0:
```python
import jax
import jax.numpy as jnp
import numpy as np
from jax import lax
from jax.sharding import PartitionSpec as P

HEAD = 128
epsilon = 1e-06


def time_embed(timesteps, feature_width):
    half_size = feature_width // 2
    freq_rate = jnp.exp(-jnp.log(10000.0) * jnp.arange(half_size, dtype=jnp.float32) / half_size)
    angles = timesteps.astype(jnp.float32)[:, None] * freq_rate[None, :]
    return jnp.concatenate([jnp.cos(angles), jnp.sin(angles)], axis=1)


def rope_tables(positions, head_size):
    first_size = head_size // 8
    other_size = (head_size - first_size) // 2
    pieces = []
    swapped = []
    sign_vec = []
    offset = 0
    for axis_id, width_part in enumerate((first_size, other_size, other_size)):
        half_size = width_part // 2
        freq_rate = jnp.exp(
            -jnp.log(256.0) * 2.0 * jnp.arange(half_size, dtype=jnp.float32) / width_part
        )
        angle_part = positions[axis_id].astype(jnp.float32)[:, None] * freq_rate[None, :]
        pieces.append(angle_part)
        pieces.append(angle_part)
        swapped += list(range(offset + half_size, offset + width_part)) + list(
            range(offset, offset + half_size)
        )
        sign_vec += [-1.0] * half_size + [1.0] * half_size
        offset += width_part
    angles = jnp.concatenate(pieces, axis=1)
    return (
        jnp.cos(angles),
        jnp.sin(angles),
        np.array(swapped, np.int32),
        np.array(sign_vec, np.float32),
    )


def rotate(values, tables):
    cos_tab, sin_tab, swapped, sign_vec = tables
    return values * cos_tab + values[..., swapped] * sign_vec * sin_tab


def unrotate(values, tables):
    cos_tab, sin_tab, swapped, sign_vec = tables
    return values * cos_tab - (values * sin_tab)[..., swapped] * sign_vec


def rms_norm(values):
    inverse = lax.rsqrt(jnp.mean(values * values, -1, keepdims=True) + epsilon)
    return (values * inverse, inverse)


def rms_back(d_normed, normed, inverse):
    return inverse * (d_normed - normed * jnp.mean(d_normed * normed, -1, keepdims=True))


def layer_norm(values):
    centred = values - jnp.mean(values, -1, keepdims=True)
    inverse_std = lax.rsqrt(jnp.mean(centred * centred, -1, keepdims=True) + epsilon)
    return (centred * inverse_std, inverse_std)


def layer_norm_back(d_normed, normed, inverse_std):
    return inverse_std * (
        d_normed
        - jnp.mean(d_normed, -1, keepdims=True)
        - normed * jnp.mean(d_normed * normed, -1, keepdims=True)
    )


def times_transposed(left, right):
    return lax.dot_general(
        left, right, (((1,), (1,)), ((), ())), preferred_element_type=jnp.float32
    )


def attend(projected, tables):
    length, groups, triple = projected.shape
    head_size = triple // 3
    grouped = jnp.transpose(projected.reshape(length, groups, 3, head_size), (2, 1, 0, 3))
    query_n, query_inv = rms_norm(grouped[0])
    key_n, key_inv = rms_norm(grouped[1])
    q_rot = rotate(query_n, tables).astype(jnp.bfloat16)
    k_rot = rotate(key_n, tables).astype(jnp.bfloat16)
    values = grouped[2].astype(jnp.bfloat16)
    score_scale = head_size ** (-0.5)
    scores = (
        jnp.einsum("gld,gmd->glm", q_rot, k_rot, preferred_element_type=jnp.float32) * score_scale
    )
    weights = jnp.exp(scores - head_size**0.5)
    probs = weights / jnp.sum(weights, -1, keepdims=True)
    probs_low = probs.astype(jnp.bfloat16)
    heads_out = jnp.einsum("glm,gmd->gld", probs_low, values, preferred_element_type=jnp.float32)
    attended = (
        jnp.transpose(heads_out, (1, 0, 2)).reshape(length, groups * head_size).astype(jnp.bfloat16)
    )
    saved = (q_rot, k_rot, values, probs, probs_low, query_n, query_inv, key_n, key_inv)
    return (attended, saved)


def attend_back(d_attended, saved, tables):
    q_rot, k_rot, values, probs, probs_low, query_n, query_inv, key_n, key_inv = saved
    groups, length, head_size = q_rot.shape
    score_scale = head_size ** (-0.5)
    d_heads = jnp.transpose(d_attended.reshape(length, groups, head_size), (1, 0, 2))
    d_values = jnp.einsum("glm,gld->gmd", probs_low, d_heads, preferred_element_type=jnp.float32)
    d_probs = jnp.einsum("gld,gmd->glm", d_heads, values, preferred_element_type=jnp.float32)
    d_scores = (probs * (d_probs - jnp.sum(probs * d_probs, -1, keepdims=True))).astype(
        jnp.bfloat16
    )
    d_qrot = (
        jnp.einsum("glm,gmd->gld", d_scores, k_rot, preferred_element_type=jnp.float32)
        * score_scale
    )
    d_krot = (
        jnp.einsum("glm,gld->gmd", d_scores, q_rot, preferred_element_type=jnp.float32)
        * score_scale
    )
    d_query = rms_back(unrotate(d_qrot, tables), query_n, query_inv)
    d_key = rms_back(unrotate(d_krot, tables), key_n, key_inv)
    stacked = jnp.stack([d_query, d_key, d_values], 0)
    return (
        jnp.transpose(stacked, (2, 1, 0, 3))
        .reshape(length, groups * 3 * head_size)
        .astype(jnp.bfloat16)
    )


def on_device(latent, timesteps, positions, mod_weight, input_weight, output_weight, cotangent):
    width = latent.shape[2]
    rows_local = latent.shape[1]
    groups = input_weight.shape[1]
    group_cols = groups * input_weight.shape[2]
    time_act = jax.nn.silu(time_embed(timesteps, width)).astype(jnp.bfloat16)
    slab_rows = mod_weight.shape[0]
    act_rows = lax.dynamic_slice_in_dim(time_act, lax.axis_index("cand") * slab_rows, slab_rows, 1)
    mod_mine = lax.psum_scatter(
        jnp.dot(act_rows, mod_weight, preferred_element_type=jnp.float32).astype(jnp.bfloat16),
        "cand",
        scatter_dimension=0,
        tiled=True,
    ).astype(jnp.float32)
    modulation = lax.all_gather(mod_mine, "seq", axis=1, tiled=True)[0]
    shift_vec = modulation[:width]
    scale_vec = modulation[width : 2 * width]
    gate_vec = modulation[2 * width :]
    latent_rows = latent[0].astype(jnp.float32)
    normed, inverse_std = layer_norm(latent_rows)
    modulated = (normed * (1.0 + scale_vec) + shift_vec).astype(jnp.bfloat16)
    gathered = lax.all_gather(modulated, "seq", axis=0, tiled=True)
    length = gathered.shape[0]
    tables = rope_tables(positions, HEAD)
    piece = lax.all_gather(input_weight, "cand", axis=0, tiled=True)
    projected = jnp.dot(
        gathered, piece.reshape(piece.shape[0], group_cols), preferred_element_type=jnp.float32
    )
    attended, saved = attend(projected.reshape(length, groups, 3 * HEAD), tables)
    w_heads = lax.all_gather(output_weight, "seq", axis=0, tiled=True)
    w_all = lax.all_gather(w_heads, "cand", axis=2, tiled=True)
    w_all = w_all.reshape(w_all.shape[0] * w_all.shape[1], width)
    token_heads = lax.all_to_all(attended, "seq", split_axis=0, concat_axis=1, tiled=True)
    mixed = jnp.dot(token_heads, w_all, preferred_element_type=jnp.float32)
    block_out = (latent_rows + gate_vec * mixed).astype(jnp.bfloat16)
    d_mixed = (cotangent[0].astype(jnp.float32) * gate_vec).astype(jnp.bfloat16)
    d_tokens = times_transposed(d_mixed, w_all).astype(jnp.bfloat16)
    d_attended = lax.all_to_all(d_tokens, "seq", split_axis=1, concat_axis=0, tiled=True)
    d_projected = attend_back(d_attended, saved, tables)
    w_back = lax.all_gather(input_weight, "cand", axis=0, tiled=True).reshape(width, group_cols)
    d_modulated = lax.psum_scatter(
        times_transposed(
            lax.slice_in_dim(d_projected, 0, rows_local * lax.axis_size("seq"), axis=0), w_back
        ).astype(jnp.bfloat16),
        "seq",
        scatter_dimension=0,
        tiled=True,
    ).astype(jnp.float32)
    latent_grad = cotangent[0].astype(jnp.float32) + layer_norm_back(
        d_modulated * (1.0 + scale_vec), normed, inverse_std
    )
    return (block_out[None], latent_grad[None])


def solution(mesh):
    placed = (
        P("cand", "seq", None),
        P(),
        P(),
        P("cand", "seq"),
        P("cand", "seq", None),
        P("seq", None, "cand"),
        P("cand", "seq", None),
    )
    return jax.shard_map(
        on_device,
        mesh=mesh,
        in_specs=placed,
        out_specs=(P("cand", "seq", None), P("cand", "seq", None)),
        check_vma=False,
    )
```

profile of v0, /device:TPU:0, one launch (start us, length us, event | category | flops | bytes accessed | tf_op | source)
XLA Modules:
  0.0 380.3 jit_solution(16041550091423698796)
XLA Ops:
  10.0 8.7 %all-reduce = bf16[4,1152]{1,0:T(4,128)(2,1)S(1)} all-reduce(bf16[4,1152]{1,0:T(4,128)(2,1)S(1)} %convolution_convert_fusion.2), channel_id=2, replica_groups=mesh['cand'=4,'seq'=8] {'cand'}, use_global_device_ids=true, to_apply=%region_0.1.clone | all-reduce | flops 4608 | bytes 18432
  19.4 31.6 %all_gather.16 = f32[1,9216]{1,0:T(1,128)S(1)} all-gather(f32[1,1152]{1,0:T(1,128)S(1)} %dynamic-slice_convert_fusion), channel_id=1, replica_groups=mesh['cand'=4,'seq'=8] {'seq'}, dimensions={1}, use_global_device_ids=true | all-gather | bytes 41472 | tf_op jit(solution)/shard_map/all_gather | solution.py:152
  52.4 20.8 %all-gather.9.cloned.1.call-done = bf16[16,128,768]{2,1,0:T(8,128)(2,1)} async-done(((bf16[2,128,768]{2,1,0:T(8,128)(2,1)}), bf16[16,128,768]{2,1,0:T(8,128)(2,1)}) %all-gather.9.cloned.1.call-update) | async-done | bytes 3145744 | tf_op jit(solution)/shard_map/all_gather | solution.py:167
  76.4 34.5 %all-gather.7.cloned.1.call-done = bf16[3072,2,384]{2,1,0:T(2,128)(2,1)} async-done(((bf16[768,2,384]{2,1,0:T(2,128)(2,1)}), bf16[3072,2,384]{2,1,0:T(2,128)(2,1)}) %all-gather.7.cloned.1.call-update) | async-done | bytes 4718608 | tf_op jit(solution)/shard_map/all_gather | solution.py:162
  110.9 5.2 %copy.89 = bf16[384,8,2,384]{3,1,2,0:T(8,128)(2,1)} copy(bf16[384,8,2,384]{3,2,1,0:T(2,128)(2,1)} %bitcast.149) | data formatting | bytes 9437184
  116.1 6.7 %copy.50 = bf16[3072,768]{0,1:T(8,128)(2,1)} copy(bf16[3072,768]{1,0:T(8,128)(2,1)} %bitcast.145) | data formatting | bytes 9437184 | tf_op jit(solution)/shard_map/reshape | solution.py:164
  122.8 42.7 %all-gather.5.cloned.1.call-done = bf16[384,3072]{1,0:T(8,128)(2,1)} async-done(((bf16[48,3072]{1,0:T(8,128)(2,1)}), bf16[384,3072]{1,0:T(8,128)(2,1)}) %all-gather.5.cloned.1.call-update) | async-done | bytes 2359312 | tf_op jit(solution)/shard_map/all_gather | solution.py:159
  165.5 5.3 %fusion.5 = f32[3,2,384,128]{2,3,0,1:T(8,128)S(1)} fusion(bf16[2,3,128,3072]{3,2,1,0:T(8,128)(2,1)} %bitcast.150, bf16[384,3072]{1,0:T(8,128)(2,1)} %all-gather.5.cloned.1.call-done), kind=kOutput, calls=%fused_computation.13 | convolution fusion | flops 1811939328 | bytes 8257536 | tf_op jit(solution)/shard_map/dot_general | solution.py:163
  171.9 75.6 %all-gather.11.cloned.1.call-done = bf16[16,128,3072]{2,1,0:T(8,128)(2,1)} async-done(((bf16[16,128,768]{2,1,0:T(8,128)(2,1)}), bf16[16,128,3072]{2,1,0:T(8,128)(2,1)}) %all-gather.11.cloned.1.call-update) | async-done | bytes 12582928 | tf_op jit(solution)/shard_map/all_gather | solution.py:168
  247.6 8.5 %convolution_convert_fusion.1 = bf16[48,2048]{1,0:T(8,128)(2,1)S(1)} fusion(bf16[2048,3072]{1,0:T(8,128)(2,1)} %bitcast.143, bf16[1,48,3072]{2,1,0:T(8,128)(2,1)S(1)} %copy-done.10, f32[3072]{0:T(1024)S(1)} %bitcast.159), kind=kOutput, calls=%fused_computation.11 | convolution fusion | flops 604520448 | bytes 13086720 | tf_op jit(solution)/shard_map/dot_general | solution.py:81
  256.7 5.5 %all-to-all-start.1 = ((bf16[48,8,256]{2,0,1:T(8,128)(2,1)}), bf16[48,8,256]{2,0,1:T(8,128)(2,1)S(1)}, u32[]{:S(2)}, u32[]{:S(2)}) async-start(bf16[48,8,256]{2,0,1:T(8,128)(2,1)} %bitcast.142), calls=%async_computation.1 | async-start | bytes 393216 | tf_op jit(solution)/shard_map/all_to_all | solution.py:175
  265.8 2.2 gather_fusion
  268.0 2.9 gather_fusion.1
  272.9 2.5 fusion.45
  275.3 2.1 multiply_reduce_fusion
  282.8 2.9 gather_fusion.3
  285.7 2.0 copy.66
  287.8 2.9 gather_fusion.2
  290.6 2.0 multiply_reduce_fusion.2
  294.9 3.5 convolution_convert_fusion
  300.2 18.7 %all_to_all.32 = bf16[8,48,256]{2,1,0:T(8,128)(2,1)S(1)} all-to-all(bf16[8,48,256]{2,1,0:T(8,128)(2,1)S(1)} %convert_element_type.131), channel_id=1, replica_groups=mesh['cand'=4,'seq'=8] {'seq'}, dimensions={0} | all-to-all | bytes 393216 | tf_op jit(solution)/shard_map/all_to_all | solution.py:170
  319.0 7.9 %fusion.2 = bf16[1,48,3072]{2,1,0:T(8,128)(2,1)} fusion(bf16[48,2048]{1,0:T(8,128)(2,1)S(1)} %bitcast.151, bf16[2048,3072]{1,0:T(8,128)(2,1)} %bitcast.144, bf16[1,48,3072]{2,1,0:T(8,128)(2,1)S(1)} %copy-done.2, f32[3072]{0:T(1024)S(1)} %bitcast.160), kind=kOutput, calls=%fused_computation.8 | convolution fusion | flops 604569600 | bytes 13381632 | tf_op jit(solution)/shard_map/dot_general | solution.py:171
  326.9 43.6 %reduce-scatter.2.cloned.1.call-done = bf16[48,3072]{1,0:T(8,128)(2,1)} async-done(((bf16[384,3072]{1,0:T(8,128)(2,1)}), bf16[48,3072]{1,0:T(8,128)(2,1)}) %reduce-scatter.2.cloned.1.call-update) | async-done | bytes 294928 | tf_op jit(solution)/shard_map/reduce_scatter | solution.py:178
  371.8 2.0 fusion.24
  (120 shorter events, 25.8 us)
Async XLA Ops:
  7.2 66.0 %all-gather.9.cloned.1.call-start = ((), (), s32[]{:S(2)}) async-start(), calls=%async_computation.5 | async-start | bytes 3538944 | tf_op jit(solution)/shard_map/all_gather | solution.py:167
  7.9 103.0 %all-gather.7.cloned.1.call-start = ((), (), s32[]{:S(2)}) async-start(), calls=%async_computation.4 | async-start | bytes 5898240 | tf_op jit(solution)/shard_map/all_gather | solution.py:162
  8.7 42.3 %copy-start.1 = (bf16[1,48,3072]{2,1,0:T(8,128)(2,1)S(1)}, bf16[1,48,3072]{2,1,0:T(8,128)(2,1)}, u32[]{:S(2)}) copy-start(bf16[1,48,3072]{2,1,0:T(8,128)(2,1)} %param.13) | copy-start | bytes 884740
  8.7 156.8 %all-gather.5.cloned.1.call-start = ((), (), s32[]{:S(2)}) async-start(), calls=%async_computation.3 | async-start | bytes 2654208 | tf_op jit(solution)/shard_map/all_gather | solution.py:159
  51.1 22.1 %copy-start.20 = (f32[48]{0:T(128)}, f32[48]{0:T(128)S(1)}, u32[]{:S(2)}) copy-start(f32[48]{0:T(128)S(1)} %broadcast_multiply_fusion.11) | copy-start | bytes 580
  51.4 21.8 %copy-start.23 = (f32[48]{0:T(128)}, f32[48]{0:T(128)S(1)}, u32[]{:S(2)}) copy-start(f32[48]{0:T(128)S(1)} %add_rsqrt_fusion.2) | copy-start | bytes 580
  51.4 196.1 %copy-start.16 = (f32[1,3072]{1,0:T(1,128)}, f32[1,3072]{1,0:T(1,128)S(1)}, u32[]{:S(2)}) copy-start(f32[1,3072]{1,0:T(1,128)S(1)} %get-tuple-element.21) | copy-start | bytes 36868
  52.4 195.2 %all-gather.11.cloned.1.call-start = ((), (), s32[]{:S(2)}) async-start(), calls=%async_computation.6 | async-start | bytes 15728640 | tf_op jit(solution)/shard_map/all_gather | solution.py:168
  165.5 82.1 %copy-start.10 = (bf16[1,48,3072]{2,1,0:T(8,128)(2,1)S(1)}, bf16[1,48,3072]{2,1,0:T(8,128)(2,1)}, u32[]{:S(2)}) copy-start(bf16[1,48,3072]{2,1,0:T(8,128)(2,1)} %param.19) | copy-start | bytes 884740
  171.9 90.5 %copy-start.18 = (f32[2,384]{1,0:T(2,128)}, f32[2,384]{1,0:T(2,128)S(1)}, u32[]{:S(2)}) copy-start(f32[2,384]{1,0:T(2,128)S(1)} %get-tuple-element.32) | copy-start | bytes 9220
  256.7 16.1 %all-to-all-start.1 = ((bf16[48,8,256]{2,0,1:T(8,128)(2,1)}), bf16[48,8,256]{2,0,1:T(8,128)(2,1)S(1)}, u32[]{:S(2)}, u32[]{:S(2)}) async-start(bf16[48,8,256]{2,0,1:T(8,128)(2,1)} %bitcast.142), calls=%async_computation.1 | async-start | bytes 393216 | tf_op jit(solution)/shard_map/all_to_all | solution.py:175
  262.2 108.2 %reduce-scatter.2.cloned.1.call-start = ((), (), s32[]{:S(2)}) async-start(), calls=%async_computation.7 | async-start | bytes 2654208 | tf_op jit(solution)/shard_map/reduce_scatter | solution.py:178
  263.7 11.7 %copy-start.3 = (f32[2,384,128]{1,2,0:T(8,128)}, f32[2,384,128]{1,2,0:T(8,128)S(1)}, u32[]{:S(2)}) copy-start(f32[2,384,128]{1,2,0:T(8,128)S(1)} %get-tuple-element.11) | copy-start | bytes 1179652
  263.7 11.7 %copy-start.4 = (f32[2,384,128]{1,2,0:T(8,128)}, f32[2,384,128]{1,2,0:T(8,128)S(1)}, u32[]{:S(2)}) copy-start(f32[2,384,128]{1,2,0:T(8,128)S(1)} %get-tuple-element.12) | copy-start | bytes 1179652
  272.8 2.5 copy-start.8
  281.8 13.1 %slice-start = ((s8[4718592]{0:T(1024)(128)(4,1)}), s8[524288]{0:T(1024)(128)(4,1)S(1)}, s32[]{:S(2)}) async-start(s8[4718592]{0:T(1024)(128)(4,1)} %bitcast.146), calls=%async_computation.8 | async-start | bytes 1048576
  282.8 7.8 %copy-start.22 = (f32[128]{0:T(128)S(1)}, f32[128]{0:T(128)}, u32[]{:S(2)}) copy-start(f32[128]{0:T(128)} %constant.63.clone) | copy-start | bytes 1540
  287.8 4.9 %copy-start.19 = (f32[2,384]{1,0:T(2,128)S(1)}, f32[2,384]{1,0:T(2,128)}, u32[]{:S(2)}) copy-start(f32[2,384]{1,0:T(2,128)} %copy-done.18) | copy-start | bytes 9220
  290.6 4.2 %slice-start.1 = ((s8[4718592]{0:T(1024)(128)(4,1)}), s8[4194304]{0:T(1024)(128)(4,1)S(1)}, s32[]{:S(2)}) async-start(s8[4718592]{0:T(1024)(128)(4,1)} %bitcast.146), calls=%async_computation.9 | async-start | bytes 8388608
  299.8 19.1 %copy-start.2 = (bf16[1,48,3072]{2,1,0:T(8,128)(2,1)S(1)}, bf16[1,48,3072]{2,1,0:T(8,128)(2,1)}, u32[]{:S(2)}) copy-start(bf16[1,48,3072]{2,1,0:T(8,128)(2,1)} %param.13) | copy-start | bytes 884740
  299.8 19.1 %copy-start.17 = (f32[1,3072]{1,0:T(1,128)S(1)}, f32[1,3072]{1,0:T(1,128)}, u32[]{:S(2)}) copy-start(f32[1,3072]{1,0:T(1,128)} %copy-done.16) | copy-start | bytes 36868
  318.9 51.6 %copy-start.21 = (f32[48]{0:T(128)S(1)}, f32[48]{0:T(128)}, u32[]{:S(2)}) copy-start(f32[48]{0:T(128)} %copy-done.20) | copy-start | bytes 580
  318.9 51.6 %copy-start.24 = (f32[48]{0:T(128)S(1)}, f32[48]{0:T(128)}, u32[]{:S(2)}) copy-start(f32[48]{0:T(128)} %copy-done.23) | copy-start | bytes 580
  318.9 52.8 %copy-start.11 = (bf16[1,48,3072]{2,1,0:T(8,128)(2,1)S(1)}, bf16[1,48,3072]{2,1,0:T(8,128)(2,1)}, u32[]{:S(2)}) copy-start(bf16[1,48,3072]{2,1,0:T(8,128)(2,1)} %param.19) | copy-start | bytes 884740
  (13 other events, 18.7 us)
Sparse Core Ops, SparseCore 0:
  10.2 62.9 all-gather.8
  74.7 36.1 all-gather.6
  113.7 51.8 all-gather.4
  166.9 80.6 all-gather.10
  298.5 71.9 reduce-scatter.1
where the time goes:
time: 381 us; the launch traced here: 380 us
  waiting for transfers between devices  219 us (57%)
  blocking collectives  59 us (15%)
  local copies, waits for them, and re-layouts  34.1 us (9%)
  matrix products  33.8 us (9%)
  other arithmetic  14.5 us (4%)
  between operations  14.3 us (4%)
  starting transfers between devices  5.89 us (2%)
    all_gather x1, waiting for transfers between devices, on_device(): w_all = lax.all_gather(w_heads, 'cand', axis=2, tiled=True)  75.6 us
    reduce_scatter x1, waiting for transfers between devices, on_device(): lax.psum_scatter(times_transposed(lax.slice_in_dim(d_projected, 0, rows_l...  43.6 us
    all_gather x1, waiting for transfers between devices, on_device(): gathered = lax.all_gather(modulated, 'seq', axis=0, tiled=True)  42.7 us
    all_gather x1, waiting for transfers between devices, on_device(): piece = lax.all_gather(input_weight, 'cand', axis=0, tiled=True)  34.5 us
    all_gather x1, blocking collectives, on_device(): modulation = lax.all_gather(mod_mine, 'seq', axis=1, tiled=True)[0]  31.6 us
    all_gather x1, waiting for transfers between devices, on_device(): w_heads = lax.all_gather(output_weight, 'seq', axis=0, tiled=True)  20.8 us
    all_to_all x1, blocking collectives, on_device(): lax.all_to_all(attended, 'seq', split_axis=0, concat_axis=1, tiled=True)  18.7 us
    dot_general x2, matrix products, times_transposed(): lax.dot_general(left, right, (((1,), (1,)), ((), ())), preferred_element_...  11.9 us
  transfers between devices with their start and end apart: 6, of which 5 were waited for; matrix products, arithmetic and copies ran while one was open for 11% of the time, Pallas kernels for 0%

commit v1 on v0

--- a/solution.py
+++ b/solution.py
@@ -6,6 +6,10 @@
 
 HEAD = 128
 epsilon = 1e-06
+
+
+def supply_all_teams_all(body):
+    return jnp.concatenate(lax.all_gather(body, "seq"), axis=1)
 
 
 def time_embed(timesteps, feature_width):
@@ -149,7 +153,7 @@
         scatter_dimension=0,
         tiled=True,
     ).astype(jnp.float32)
-    modulation = lax.all_gather(mod_mine, "seq", axis=1, tiled=True)[0]
+    modulation = supply_all_teams_all(mod_mine)[0]
     shift_vec = modulation[:width]
     scale_vec = modulation[width : 2 * width]
     gate_vec = modulation[2 * width :]

time: 381 us -> 381 us (level)
  no operation moved by 1% of the time
where the time goes in v1:
time: 381 us; the launch traced here: 380 us
  waiting for transfers between devices  219 us (57%)
  blocking collectives  59 us (15%)
  local copies, waits for them, and re-layouts  34.1 us (9%)
  matrix products  33.8 us (9%)
  other arithmetic  14.5 us (4%)
  between operations  14.3 us (4%)
  starting transfers between devices  5.89 us (2%)
    all_gather x1, waiting for transfers between devices, on_device(): w_all = lax.all_gather(w_heads, 'cand', axis=2, tiled=True)  75.6 us
    reduce_scatter x1, waiting for transfers between devices, on_device(): lax.psum_scatter(times_transposed(lax.slice_in_dim(d_projected, 0, rows_l...  43.6 us
    all_gather x1, waiting for transfers between devices, on_device(): gathered = lax.all_gather(modulated, 'seq', axis=0, tiled=True)  42.7 us
    all_gather x1, waiting for transfers between devices, on_device(): piece = lax.all_gather(input_weight, 'cand', axis=0, tiled=True)  34.5 us
    all_gather x1, blocking collectives, supply_all_teams_all(): return jnp.concatenate(lax.all_gather(body, 'seq'), axis=1)  31.6 us
    all_gather x1, waiting for transfers between devices, on_device(): w_heads = lax.all_gather(output_weight, 'seq', axis=0, tiled=True)  20.8 us
    all_to_all x1, blocking collectives, on_device(): lax.all_to_all(attended, 'seq', split_axis=0, concat_axis=1, tiled=True)  18.7 us
    dot_general x2, matrix products, times_transposed(): lax.dot_general(left, right, (((1,), (1,)), ((), ())), preferred_element_...  11.9 us
  transfers between devices with their start and end apart: 6, of which 5 were waited for; matrix products, arithmetic and copies ran while one was open for 11% of the time, Pallas kernels for 0%

profile of v1, /device:TPU:0, one launch (start us, length us, event | category | flops | bytes accessed | tf_op | source)
XLA Modules:
  0.0 380.3 jit_solution(220136956483584241)
XLA Ops:
  10.0 8.7 %all-reduce = bf16[4,1152]{1,0:T(4,128)(2,1)S(1)} all-reduce(bf16[4,1152]{1,0:T(4,128)(2,1)S(1)} %convolution_convert_fusion.2), channel_id=3, replica_groups=mesh['cand'=4,'seq'=8] {'cand'}, use_global_device_ids=true, to_apply=%region_0.1.clone | all-reduce | flops 4608 | bytes 18432
  19.4 31.6 %all-gather.1 = f32[8,1,1152]{2,1,0:T(1,128)S(1)} all-gather(f32[1,1,1152]{2,1,0:T(1,128)S(1)} %bitcast_convert_fusion), channel_id=2, replica_groups=mesh['cand'=4,'seq'=8] {'seq'}, dimensions={0}, use_global_device_ids=true | all-gather | bytes 41472 | tf_op jit(solution)/shard_map/all_gather | solution.py:12
  52.4 20.8 %all-gather.11.cloned.1.call-done = bf16[16,128,768]{2,1,0:T(8,128)(2,1)} async-done(((bf16[2,128,768]{2,1,0:T(8,128)(2,1)}), bf16[16,128,768]{2,1,0:T(8,128)(2,1)}) %all-gather.11.cloned.1.call-update) | async-done | bytes 3145744 | tf_op jit(solution)/shard_map/all_gather | solution.py:171
  76.4 34.5 %all-gather.9.cloned.1.call-done = bf16[3072,2,384]{2,1,0:T(2,128)(2,1)} async-done(((bf16[768,2,384]{2,1,0:T(2,128)(2,1)}), bf16[3072,2,384]{2,1,0:T(2,128)(2,1)}) %all-gather.9.cloned.1.call-update) | async-done | bytes 4718608 | tf_op jit(solution)/shard_map/all_gather | solution.py:166
  110.9 5.2 %copy.89 = bf16[384,8,2,384]{3,1,2,0:T(8,128)(2,1)} copy(bf16[384,8,2,384]{3,2,1,0:T(2,128)(2,1)} %bitcast.150) | data formatting | bytes 9437184
  116.1 6.7 %copy.50 = bf16[3072,768]{0,1:T(8,128)(2,1)} copy(bf16[3072,768]{1,0:T(8,128)(2,1)} %bitcast.146) | data formatting | bytes 9437184 | tf_op jit(solution)/shard_map/reshape | solution.py:168
  122.8 42.7 %all-gather.7.cloned.1.call-done = bf16[384,3072]{1,0:T(8,128)(2,1)} async-done(((bf16[48,3072]{1,0:T(8,128)(2,1)}), bf16[384,3072]{1,0:T(8,128)(2,1)}) %all-gather.7.cloned.1.call-update) | async-done | bytes 2359312 | tf_op jit(solution)/shard_map/all_gather | solution.py:163
  165.5 5.3 %fusion.5 = f32[3,2,384,128]{2,3,0,1:T(8,128)S(1)} fusion(bf16[2,3,128,3072]{3,2,1,0:T(8,128)(2,1)} %bitcast.151, bf16[384,3072]{1,0:T(8,128)(2,1)} %all-gather.7.cloned.1.call-done), kind=kOutput, calls=%fused_computation.13 | convolution fusion | flops 1811939328 | bytes 8257536 | tf_op jit(solution)/shard_map/dot_general | solution.py:167
  171.9 75.6 %all-gather.13.cloned.1.call-done = bf16[16,128,3072]{2,1,0:T(8,128)(2,1)} async-done(((bf16[16,128,768]{2,1,0:T(8,128)(2,1)}), bf16[16,128,3072]{2,1,0:T(8,128)(2,1)}) %all-gather.13.cloned.1.call-update) | async-done | bytes 12582928 | tf_op jit(solution)/shard_map/all_gather | solution.py:172
  247.6 8.5 %convolution_convert_fusion.1 = bf16[48,2048]{1,0:T(8,128)(2,1)S(1)} fusion(bf16[2048,3072]{1,0:T(8,128)(2,1)} %bitcast.144, bf16[1,48,3072]{2,1,0:T(8,128)(2,1)S(1)} %copy-done.10, f32[3072]{0:T(1024)S(1)} %get-tuple-element.21), kind=kOutput, calls=%fused_computation.11 | convolution fusion | flops 604520448 | bytes 13086720 | tf_op jit(solution)/shard_map/dot_general | solution.py:85
  256.7 5.5 %all-to-all-start.1 = ((bf16[48,8,256]{2,0,1:T(8,128)(2,1)}), bf16[48,8,256]{2,0,1:T(8,128)(2,1)S(1)}, u32[]{:S(2)}, u32[]{:S(2)}) async-start(bf16[48,8,256]{2,0,1:T(8,128)(2,1)} %bitcast.143), calls=%async_computation.1 | async-start | bytes 393216 | tf_op jit(solution)/shard_map/all_to_all | solution.py:179
  265.8 2.2 gather_fusion
  268.0 2.9 gather_fusion.1
  272.9 2.5 fusion.45
  275.3 2.1 multiply_reduce_fusion
  282.8 2.9 gather_fusion.3
  285.7 2.0 copy.66
  287.8 2.9 gather_fusion.2
  290.6 2.0 multiply_reduce_fusion.2
  294.9 3.5 convolution_convert_fusion
  300.2 18.7 %all_to_all.32 = bf16[8,48,256]{2,1,0:T(8,128)(2,1)S(1)} all-to-all(bf16[8,48,256]{2,1,0:T(8,128)(2,1)S(1)} %convert_element_type.128), channel_id=1, replica_groups=mesh['cand'=4,'seq'=8] {'seq'}, dimensions={0} | all-to-all | bytes 393216 | tf_op jit(solution)/shard_map/all_to_all | solution.py:174
  319.0 7.9 %fusion.2 = bf16[1,48,3072]{2,1,0:T(8,128)(2,1)} fusion(bf16[48,2048]{1,0:T(8,128)(2,1)S(1)} %bitcast.152, bf16[2048,3072]{1,0:T(8,128)(2,1)} %bitcast.145, bf16[1,48,3072]{2,1,0:T(8,128)(2,1)S(1)} %copy-done.2, f32[3072]{0:T(1024)S(1)} %copy-done.17), kind=kOutput, calls=%fused_computation.8 | convolution fusion | flops 604569600 | bytes 13381632 | tf_op jit(solution)/shard_map/dot_general | solution.py:175
  326.9 43.6 %reduce-scatter.2.cloned.1.call-done = bf16[48,3072]{1,0:T(8,128)(2,1)} async-done(((bf16[384,3072]{1,0:T(8,128)(2,1)}), bf16[48,3072]{1,0:T(8,128)(2,1)}) %reduce-scatter.2.cloned.1.call-update) | async-done | bytes 294928 | tf_op jit(solution)/shard_map/reduce_scatter | solution.py:182
  371.8 2.0 fusion.24
  (120 shorter events, 25.8 us)
Async XLA Ops:
  7.2 66.0 %all-gather.11.cloned.1.call-start = ((), (), s32[]{:S(2)}) async-start(), calls=%async_computation.5 | async-start | bytes 3538944 | tf_op jit(solution)/shard_map/all_gather | solution.py:171
  7.9 103.0 %all-gather.9.cloned.1.call-start = ((), (), s32[]{:S(2)}) async-start(), calls=%async_computation.4 | async-start | bytes 5898240 | tf_op jit(solution)/shard_map/all_gather | solution.py:166
  8.7 42.3 %copy-start.1 = (bf16[1,48,3072]{2,1,0:T(8,128)(2,1)S(1)}, bf16[1,48,3072]{2,1,0:T(8,128)(2,1)}, u32[]{:S(2)}) copy-start(bf16[1,48,3072]{2,1,0:T(8,128)(2,1)} %param.13) | copy-start | bytes 884740
  8.7 156.8 %all-gather.7.cloned.1.call-start = ((), (), s32[]{:S(2)}) async-start(), calls=%async_computation.3 | async-start | bytes 2654208 | tf_op jit(solution)/shard_map/all_gather | solution.py:163
  51.1 22.1 %copy-start.20 = (f32[48]{0:T(128)}, f32[48]{0:T(128)S(1)}, u32[]{:S(2)}) copy-start(f32[48]{0:T(128)S(1)} %broadcast_multiply_fusion.11) | copy-start | bytes 580
  51.4 21.8 %copy-start.23 = (f32[48]{0:T(128)}, f32[48]{0:T(128)S(1)}, u32[]{:S(2)}) copy-start(f32[48]{0:T(128)S(1)} %add_rsqrt_fusion.2) | copy-start | bytes 580
  51.4 196.1 %copy-start.16 = (f32[3072]{0:T(1024)}, f32[3072]{0:T(1024)S(1)}, u32[]{:S(2)}) copy-start(f32[3072]{0:T(1024)S(1)} %get-tuple-element.21) | copy-start | bytes 36868
  52.4 195.2 %all-gather.13.cloned.1.call-start = ((), (), s32[]{:S(2)}) async-start(), calls=%async_computation.6 | async-start | bytes 15728640 | tf_op jit(solution)/shard_map/all_gather | solution.py:172
  165.5 82.1 %copy-start.10 = (bf16[1,48,3072]{2,1,0:T(8,128)(2,1)S(1)}, bf16[1,48,3072]{2,1,0:T(8,128)(2,1)}, u32[]{:S(2)}) copy-start(bf16[1,48,3072]{2,1,0:T(8,128)(2,1)} %param.19) | copy-start | bytes 884740
  171.9 90.5 %copy-start.18 = (f32[2,384]{1,0:T(2,128)}, f32[2,384]{1,0:T(2,128)S(1)}, u32[]{:S(2)}) copy-start(f32[2,384]{1,0:T(2,128)S(1)} %get-tuple-element.32) | copy-start | bytes 9220
  256.7 16.1 %all-to-all-start.1 = ((bf16[48,8,256]{2,0,1:T(8,128)(2,1)}), bf16[48,8,256]{2,0,1:T(8,128)(2,1)S(1)}, u32[]{:S(2)}, u32[]{:S(2)}) async-start(bf16[48,8,256]{2,0,1:T(8,128)(2,1)} %bitcast.143), calls=%async_computation.1 | async-start | bytes 393216 | tf_op jit(solution)/shard_map/all_to_all | solution.py:179
  262.2 108.2 %reduce-scatter.2.cloned.1.call-start = ((), (), s32[]{:S(2)}) async-start(), calls=%async_computation.7 | async-start | bytes 2654208 | tf_op jit(solution)/shard_map/reduce_scatter | solution.py:182
  263.7 11.7 %copy-start.3 = (f32[2,384,128]{1,2,0:T(8,128)}, f32[2,384,128]{1,2,0:T(8,128)S(1)}, u32[]{:S(2)}) copy-start(f32[2,384,128]{1,2,0:T(8,128)S(1)} %get-tuple-element.11) | copy-start | bytes 1179652
  263.7 11.7 %copy-start.4 = (f32[2,384,128]{1,2,0:T(8,128)}, f32[2,384,128]{1,2,0:T(8,128)S(1)}, u32[]{:S(2)}) copy-start(f32[2,384,128]{1,2,0:T(8,128)S(1)} %get-tuple-element.12) | copy-start | bytes 1179652
  272.8 2.5 copy-start.8
  281.8 13.1 %slice-start = ((s8[4718592]{0:T(1024)(128)(4,1)}), s8[524288]{0:T(1024)(128)(4,1)S(1)}, s32[]{:S(2)}) async-start(s8[4718592]{0:T(1024)(128)(4,1)} %bitcast.147), calls=%async_computation.8 | async-start | bytes 1048576
  282.8 7.8 %copy-start.22 = (f32[128]{0:T(128)S(1)}, f32[128]{0:T(128)}, u32[]{:S(2)}) copy-start(f32[128]{0:T(128)} %constant.63.clone) | copy-start | bytes 1540
  287.8 4.9 %copy-start.19 = (f32[2,384]{1,0:T(2,128)S(1)}, f32[2,384]{1,0:T(2,128)}, u32[]{:S(2)}) copy-start(f32[2,384]{1,0:T(2,128)} %copy-done.18) | copy-start | bytes 9220
  290.6 4.2 %slice-start.1 = ((s8[4718592]{0:T(1024)(128)(4,1)}), s8[4194304]{0:T(1024)(128)(4,1)S(1)}, s32[]{:S(2)}) async-start(s8[4718592]{0:T(1024)(128)(4,1)} %bitcast.147), calls=%async_computation.9 | async-start | bytes 8388608
  299.8 19.1 %copy-start.2 = (bf16[1,48,3072]{2,1,0:T(8,128)(2,1)S(1)}, bf16[1,48,3072]{2,1,0:T(8,128)(2,1)}, u32[]{:S(2)}) copy-start(bf16[1,48,3072]{2,1,0:T(8,128)(2,1)} %param.13) | copy-start | bytes 884740
  299.8 19.1 %copy-start.17 = (f32[3072]{0:T(1024)S(1)}, f32[3072]{0:T(1024)}, u32[]{:S(2)}) copy-start(f32[3072]{0:T(1024)} %copy-done.16) | copy-start | bytes 36868
  318.9 51.6 %copy-start.21 = (f32[48]{0:T(128)S(1)}, f32[48]{0:T(128)}, u32[]{:S(2)}) copy-start(f32[48]{0:T(128)} %copy-done.20) | copy-start | bytes 580
  318.9 51.6 %copy-start.24 = (f32[48]{0:T(128)S(1)}, f32[48]{0:T(128)}, u32[]{:S(2)}) copy-start(f32[48]{0:T(128)} %copy-done.23) | copy-start | bytes 580
  318.9 52.8 %copy-start.11 = (bf16[1,48,3072]{2,1,0:T(8,128)(2,1)S(1)}, bf16[1,48,3072]{2,1,0:T(8,128)(2,1)}, u32[]{:S(2)}) copy-start(bf16[1,48,3072]{2,1,0:T(8,128)(2,1)} %param.19) | copy-start | bytes 884740
  (13 other events, 18.7 us)
Sparse Core Ops, SparseCore 0:
  10.2 62.9 all-gather.10
  74.7 36.1 all-gather.8
  113.7 51.8 all-gather.6
  166.9 80.6 all-gather.12
  298.5 71.9 reduce-scatter.1
